TPU v7x, 256 devices: a whole 4x4x8 slice. The times are simulated.
256 devices in a mesh: lat: 8 (over z_hi, core), lon: 32 (over x, z_lo, y).
Axes of the slice: x: 4, y: 4, z: 8 (z_hi: 4, z_lo: 2; z = z_hi * 2 + z_lo), core: 2. Of those that a mesh axis runs over, the one named last changes fastest.
Arguments:
- forcing: bfloat16 [16, 128, 4096], P(None, 'lat', 'lon'), may hold values from -6 to 6
- hidden: bfloat16 [64, 128, 4096], P(None, 'lat', 'lon'), may hold values from -3 to 3
- cell: bfloat16 [64, 128, 4096], P(None, 'lat', 'lon'), may hold values from -6 to 6
- grad_hidden: bfloat16 [64, 128, 4096], P(None, 'lat', 'lon'), may hold values from -6 to 6
- grad_cell: bfloat16 [64, 128, 4096], P(None, 'lat', 'lon'), may hold values from -6 to 6
- wet_mask: int32 [8, 256], P('lat'), may hold values from 0 to 1
- tile_owner: int32 [8, 256], P('lat'), may hold values from 0 to 31, as said below
- w_gates: bfloat16 [256, 720], replicated, may hold values from -0.21875 to 0.21875
- b_gates: float32 [256], replicated, may hold values from -3 to 3
Outputs:
- hidden_next: bfloat16 [64, 128, 4096], P(None, 'lat', 'lon')
- cell_next: float32 [1024, 64, 256], P(('lat', 'lon'))
- hidden_grad: float32 [64, 128, 4096], P(None, 'lat', 'lon')
- cell_grad: float32 [64, 128, 4096], P(None, 'lat', 'lon')
- weight_grad: float32 [256, 720], replicated
- bias_grad: float32 [256], replicated
Inputs may be any that keep to these rules, and one draw needn't show every extreme that they name: Within each group of 1 tile rows, tile_owner gives every longitude index exactly 4 wet tiles, and gives the wet tiles of one longitude block of 8 tile columns at most 1 to any one index; both bounds are reached in every draw, and some block is wet throughout. Dry tiles carry an owner too.
All inputs are finite; a program needn't handle non-finite values.
Results may differ from a plain program's by a relative error of at most 0.0033.
Values may be sent and summed in bfloat16 or wider, within the bound.
A program may use at most 64 MiB of HBM per device.

v0:
```python
import math

import jax
import jax.numpy as jnp
from jax import lax
from jax.sharding import PartitionSpec as P

TILE = 16


def extended_2(cells, sides, width):
    for axis, dim in sides:
        count = lax.axis_size(axis)
        head = lax.slice_in_dim(cells, 0, width, axis=dim)
        tail = lax.slice_in_dim(cells, cells.shape[dim] - width, cells.shape[dim], axis=dim)
        cells = jnp.concatenate(
            [
                lax.ppermute(tail, axis, [(i, (i + 1) % count) for i in range(count)]),
                cells,
                lax.ppermute(head, axis, [((i + 1) % count, i) for i in range(count)]),
            ],
            axis=dim,
        )
    return cells


def last_pad(values_in, pad_front, pad_back):
    widths = [(0, 0)] * (values_in.ndim - 1) + [(pad_front, pad_back)]
    return jnp.pad(values_in, widths)


def fold_edges(values_in):
    tile_count = values_in.shape[-2]
    inner_size = values_in.shape[-1] - 2
    leading = values_in.shape[:-2]
    flat_shape = leading + (tile_count * inner_size,)
    middle = values_in[..., 1 : inner_size + 1].reshape(flat_shape)
    zeros_left = jnp.zeros(leading + (tile_count, inner_size - 1), values_in.dtype)
    left_edge = jnp.concatenate([values_in[..., 0:1], zeros_left], -1).reshape(flat_shape)
    zeros_one = jnp.zeros(leading + (tile_count, 1), values_in.dtype)
    zeros_rest = jnp.zeros(leading + (tile_count, inner_size - 2), values_in.dtype)
    right_edge = jnp.concatenate(
        [zeros_one, values_in[..., inner_size + 1 : inner_size + 2], zeros_rest], -1
    ).reshape(flat_shape)
    full_size = tile_count * inner_size + 2
    return (
        last_pad(middle, 1, 1)
        + last_pad(left_edge, 0, 2)
        + last_pad(right_edge, inner_size, 0)[..., :full_size]
    )


def lstm_terms(pre_in, pre_forget, pre_out, pre_cand, cell_in, hidden_cot, cell_cot, live_cells):
    gate_in = jax.nn.sigmoid(pre_in)
    gate_forget = jax.nn.sigmoid(pre_forget)
    gate_out = jax.nn.sigmoid(pre_out)
    candidate = jnp.tanh(pre_cand)
    cell_new = gate_forget * cell_in + gate_in * candidate
    squash = jnp.tanh(cell_new)
    hidden_new = (live_cells * gate_out * squash).astype(jnp.bfloat16)
    back_h = live_cells * hidden_cot.astype(jnp.float32)
    back_c = live_cells * cell_cot.astype(jnp.float32) + back_h * gate_out * (1.0 - squash * squash)
    cell_back = back_c * gate_forget
    delta_parts = (
        back_c * candidate * gate_in * (1.0 - gate_in),
        back_c * cell_in * gate_forget * (1.0 - gate_forget),
        back_h * squash * gate_out * (1.0 - gate_out),
        back_c * gate_in * (1.0 - candidate * candidate),
    )
    return (hidden_new, cell_new, cell_back, delta_parts)


def tile_step(slab_tiles, cell_tiles, hidden_cot, cell_cot, live_tiles, w_gates, b_gates):
    tile_count = slab_tiles.shape[0]
    channels = slab_tiles.shape[1]
    hid_count = cell_tiles.shape[1]
    side_cells = TILE
    tile_grid = slab_tiles.reshape(tile_count, channels, side_cells + 2, side_cells + 2)
    tap_list = []
    for row_off in range(3):
        for col_off in range(3):
            tap_list.append(
                tile_grid[
                    :, :, row_off : row_off + side_cells, col_off : col_off + side_cells
                ].reshape(tile_count, channels, side_cells * side_cells)
            )
    patches = jnp.concatenate(tap_list, 1)
    pre_gates = (
        jnp.einsum("gk,nkc->ngc", w_gates, patches, preferred_element_type=jnp.float32)
        + b_gates[None, :, None]
    )
    live_cells = live_tiles[:, None, None]
    hidden_new, cell_new, cell_back, delta_parts = lstm_terms(
        pre_gates[:, :hid_count],
        pre_gates[:, hid_count : 2 * hid_count],
        pre_gates[:, 2 * hid_count : 3 * hid_count],
        pre_gates[:, 3 * hid_count :],
        cell_tiles.astype(jnp.float32),
        hidden_cot,
        cell_cot,
        live_cells,
    )
    gate_delta = jnp.concatenate(delta_parts, 1).astype(jnp.bfloat16)
    weight_part = jnp.einsum("ngc,nkc->gk", gate_delta, patches, preferred_element_type=jnp.float32)
    bias_part = jnp.sum(gate_delta.astype(jnp.float32), axis=(0, 2))
    hid_weights = w_gates.reshape(w_gates.shape[0], 9, channels)[:, :, channels - hid_count :]
    spread = jnp.einsum(
        "gth,ngc->nthc", hid_weights, gate_delta, preferred_element_type=jnp.float32
    )
    grad_pad = jnp.zeros((tile_count, hid_count, side_cells + 2, side_cells + 2), jnp.float32)
    for row_off in range(3):
        for col_off in range(3):
            placed = spread[:, row_off * 3 + col_off].reshape(
                tile_count, hid_count, side_cells, side_cells
            )
            grad_pad = grad_pad + jnp.pad(
                placed, ((0, 0), (0, 0), (row_off, 2 - row_off), (col_off, 2 - col_off))
            )
    grad_pad = grad_pad.reshape(tile_count, hid_count, (side_cells + 2) * (side_cells + 2))
    return (hidden_new, cell_new, cell_back, grad_pad, weight_part, bias_part)


def outside_rows(row_total, lat_index, lat_devices):
    position = jnp.arange(row_total, dtype=jnp.int32)
    upper = (position == 0) & (lat_index == 0)
    lower = (position == row_total - 1) & (lat_index == lat_devices - 1)
    return jnp.where(upper | lower, 0.0, 1.0).astype(jnp.float32)


def cut_tiles(padded, tile_rows, tile_cols):
    channels = padded.shape[0]
    side_cells = TILE + 2
    row_pick = (
        jnp.arange(tile_rows, dtype=jnp.int32)[:, None] * TILE
        + jnp.arange(side_cells, dtype=jnp.int32)[None, :]
    ).reshape(-1)
    col_pick = (
        jnp.arange(tile_cols, dtype=jnp.int32)[:, None] * TILE
        + jnp.arange(side_cells, dtype=jnp.int32)[None, :]
    ).reshape(-1)
    strips = jnp.take(padded, row_pick, axis=1).reshape(
        channels, tile_rows, side_cells, padded.shape[2]
    )
    pieces = jnp.take(strips, col_pick, axis=3).reshape(
        channels, tile_rows, side_cells, tile_cols, side_cells
    )
    return jnp.transpose(pieces, (1, 3, 0, 2, 4)).reshape(
        tile_rows * tile_cols, channels, side_cells * side_cells
    )


def to_tiles(values_in, tile_rows, tile_cols):
    channels = values_in.shape[0]
    shaped = values_in.reshape(channels, tile_rows, TILE, tile_cols, TILE)
    return jnp.transpose(shaped, (1, 3, 0, 2, 4)).reshape(
        tile_rows * tile_cols, channels, TILE * TILE
    )


def from_tiles(tiles_in, tile_rows, tile_cols):
    channels = tiles_in.shape[1]
    shaped = tiles_in.reshape(tile_rows, tile_cols, channels, TILE, TILE)
    return jnp.transpose(shaped, (2, 0, 3, 1, 4)).reshape(
        channels, tile_rows * TILE, tile_cols * TILE
    )


def sender_plan(wet_local, dest_local, slot_count, pair_most):
    tile_count = wet_local.shape[0]
    position = jnp.arange(tile_count, dtype=jnp.int32)
    earlier = position[:, None] < position[None, :]
    same_dest = (
        (dest_local[:, None] == dest_local[None, :]) & wet_local[:, None] & wet_local[None, :]
    )
    dest_rank = jnp.sum((same_dest & earlier).astype(jnp.int32), 0)
    slot_of = dest_local * pair_most + dest_rank
    placed = wet_local[:, None] & (
        slot_of[:, None] == jnp.arange(slot_count, dtype=jnp.int32)[None, :]
    )
    source = jnp.sum(placed.astype(jnp.int32) * position[:, None], 0)
    filled = jnp.any(placed, 0)
    send_index = jnp.where(filled, source, tile_count)
    home_index = jnp.where(wet_local, slot_of, slot_count)
    return (send_index, home_index)


def receiver_plan(arrivals, pair_most, capacity):
    slot_count = arrivals.shape[0] * pair_most
    positions = jnp.arange(slot_count, dtype=jnp.int32)
    filled = positions % pair_most < jnp.repeat(arrivals, pair_most)
    slot_rank = jnp.cumsum(filled.astype(jnp.int32)) - 1
    placed = filled[None, :] & (
        slot_rank[None, :] == jnp.arange(capacity, dtype=jnp.int32)[:, None]
    )
    work_index = jnp.sum(placed.astype(jnp.int32) * positions[None, :], 1)
    back_index = jnp.where(filled, slot_rank, capacity)
    return (work_index, back_index)


def pick_rows(arrays, row_index):
    picked = []
    for member in arrays:
        extended = jnp.concatenate([member, jnp.zeros((1,) + member.shape[1:], member.dtype)], 0)
        picked.append(jnp.take(extended, row_index, axis=0))
    return tuple(picked)


def fold_grad(pad_tiles, tile_rows, tile_cols, row_keep):
    hid_count = pad_tiles.shape[1]
    side_cells = TILE + 2
    shaped = pad_tiles.reshape(tile_rows, tile_cols, hid_count, side_cells, side_cells)
    across = fold_edges(jnp.transpose(shaped, (0, 2, 3, 1, 4)))
    down_fold = fold_edges(jnp.transpose(across, (1, 3, 0, 2)))
    overhang = jnp.transpose(down_fold, (0, 2, 1)) * row_keep[None, :, None]
    received = extended_2(overhang, (("lat", 1), ("lon", 2)), 1)
    lat_size = overhang.shape[1] - 2
    lon_size = overhang.shape[2] - 2
    columns = received[:, :, 2 : lon_size + 2]
    columns = columns.at[:, :, 0].add(received[:, :, 0])
    columns = columns.at[:, :, lon_size - 1].add(received[:, :, lon_size + 3])
    result = columns[:, 2 : lat_size + 2]
    result = result.at[:, 0].add(columns[:, 0])
    result = result.at[:, lat_size - 1].add(columns[:, lat_size + 3])
    return result


def body(forcing, hidden, cell, grad_hidden, grad_cell, wet_mask, tile_owner, w_gates, b_gates):
    lat_index = lax.axis_index("lat")
    lon_index = lax.axis_index("lon")
    lat_devices = lax.axis_size("lat")
    lon_devices = lax.axis_size("lon")
    tile_rows = wet_mask.shape[0]
    tile_cols = wet_mask.shape[1] // lon_devices
    tile_count = tile_rows * tile_cols
    pair_most = max(1, tile_count // lon_devices)
    slot_count = lon_devices * pair_most
    capacity = tile_count // 2
    fields = jnp.concatenate([forcing, hidden], 0)
    padded = extended_2(fields, (("lat", 1), ("lon", 2)), 1)
    row_keep = outside_rows(padded.shape[1], lat_index, lat_devices)
    padded = padded * row_keep.astype(jnp.bfloat16)[None, :, None]
    slab_tiles = cut_tiles(padded, tile_rows, tile_cols)
    cell_tiles = to_tiles(cell, tile_rows, tile_cols)
    hidden_cot = to_tiles(grad_hidden, tile_rows, tile_cols)
    cell_cot = to_tiles(grad_cell, tile_rows, tile_cols)
    wet_local = (
        lax.dynamic_slice_in_dim(wet_mask, lon_index * tile_cols, tile_cols, 1).reshape(tile_count)
        > 0
    )
    dest_local = lax.dynamic_slice_in_dim(tile_owner, lon_index * tile_cols, tile_cols, 1).reshape(
        tile_count
    )
    send_index, home_index = sender_plan(wet_local, dest_local, slot_count, pair_most)
    owned_here = (wet_mask > 0) & (tile_owner == lon_index)
    arrivals = jnp.sum(
        owned_here.reshape(tile_rows, lon_devices, tile_cols).astype(jnp.int32), axis=(0, 2)
    )
    work_index, back_index = receiver_plan(arrivals, pair_most, capacity)
    hid_tiles, cell_new, back_tiles, pad_tiles, weight_part, bias_part = tile_step(
        slab_tiles,
        cell_tiles,
        hidden_cot,
        cell_cot,
        wet_local.astype(jnp.float32),
        w_gates,
        b_gates,
    )
    outgoing_state = pick_rows((cell_new,), send_index)[0]
    incoming_state = lax.all_to_all(outgoing_state, "lon", split_axis=0, concat_axis=0, tiled=True)
    cell_next = pick_rows((incoming_state,), work_index)[0]
    hidden_next = from_tiles(hid_tiles, tile_rows, tile_cols)
    cell_grad = from_tiles(back_tiles, tile_rows, tile_cols)
    hidden_grad = fold_grad(pad_tiles, tile_rows, tile_cols, row_keep)
    totals = lax.psum((weight_part, bias_part), ("lat", "lon"))
    scaling = 1.0 / math.sqrt(float(lat_devices * lon_devices * capacity * TILE * TILE))
    return (
        hidden_next,
        cell_next,
        hidden_grad,
        cell_grad,
        totals[0] * scaling,
        totals[1] * scaling,
    )


def solution(mesh):
    return jax.shard_map(
        body,
        mesh=mesh,
        in_specs=(
            P(None, "lat", "lon"),
            P(None, "lat", "lon"),
            P(None, "lat", "lon"),
            P(None, "lat", "lon"),
            P(None, "lat", "lon"),
            P("lat", None),
            P("lat", None),
            P(),
            P(),
        ),
        out_specs=(
            P(None, "lat", "lon"),
            P(("lat", "lon"), None, None),
            P(None, "lat", "lon"),
            P(None, "lat", "lon"),
            P(),
            P(),
        ),
        check_vma=False,
    )
```

profile of v0, /device:TPU:1, one launch (start us, length us, event | category | flops | bytes accessed | tf_op | source)
XLA Modules:
  0.0 353.8 jit_solution(3883284366061151006)
XLA Ops:
  9.8 4.4 %collective-permute-start = (bf16[80,1,128]{0,2,1:T(8,128)(2,1)S(1)}, bf16[80,1,128]{0,2,1:T(8,128)(2,1)S(1)}, u32[]{:S(2)}, u32[]{:S(2)}) collective-permute-start(bf16[80,1,128]{0,2,1:T(8,128)(2,1)S(1)} %get-tuple-element.99), channel_id=1, source_target_pairs={{0,32},{32,64},{64,96},{96,128},{128,160},{160,192},{192,224},{224... | collective-permute-start | bytes 61448 | tf_op jit(solution)/shard_map/ppermute | solution.py:18
  21.4 5.3 %collective-permute-start.3 = (bf16[80,18,1]{0,2,1:T(2,128)(2,1)S(1)}, bf16[80,18,1]{0,2,1:T(2,128)(2,1)S(1)}, u32[]{:S(2)}, u32[]{:S(2)}) collective-permute-start(bf16[80,18,1]{0,2,1:T(2,128)(2,1)S(1)} %get-tuple-element.98), channel_id=1, source_target_pairs={{1,0},{2,1},{3,2},{4,3},{5,4},{6,5},{7,6},{8,7},{9,8},{10,9},{11,1... | collective-permute-start | bytes 8648 | tf_op jit(solution)/shard_map/ppermute | solution.py:20
  29.3 2.3 copy.109
  34.3 2.4 copy.107
  39.2 2.0 fusion.35
  45.1 2.0 copy.97
  48.9 2.0 copy.96
  52.8 2.0 copy.95
  56.6 2.0 copy.94
  59.4 2.0 copy.93
  75.4 4.4 %all-to-all-start = ((f32[32,64,256]{2,1,0:T(8,128)}), f32[32,64,256]{2,1,0:T(8,128)S(1)}, u32[]{:S(2)}, u32[]{:S(2)}) async-start(f32[32,64,256]{2,1,0:T(8,128)} %broadcast_select_fusion), calls=%async_computation | async-start | bytes 4194304 | tf_op jit(solution)/shard_map/all_to_all | solution.py:269
  81.6 2.2 fusion.32
  85.2 2.3 copy.120
  87.5 2.4 copy.119
  89.9 2.4 copy.118
  92.3 2.4 copy.117
  94.7 2.4 copy.116
  97.1 2.4 copy.115
  99.5 2.4 copy.114
  101.9 2.4 copy.113
  104.3 4.7 %add_bitcast_fusion.1 = f32[1,64,18,8,18]{1,4,2,3,0:T(8,128)S(1)} fusion(f32[8,64,16,16]{1,3,2,0:T(8,128)} %bitcast.122, f32[8,64,16,16]{1,3,2,0:T(8,128)} %bitcast.123, f32[8,64,16,16]{1,3,2,0:T(8,128)} %bitcast.124, f32[8,64,16,16]{1,3,2,0:T(8,128)} %bitcast.125, f32[8,64,16,16]{1,3,2,0:T(8,128)} %bitcast.126, f32[8,64,16,16]{1,3,2,0:T(8,128)} %bitcast.127, ...), kind=kLoop, calls=%fused_computation.8 | loop fusion | flops 1327104 | bytes 5382144 | tf_op jit(solution)/shard_map/transpose | solution.py:212
  111.3 2.9 collective-permute-start.4
  114.5 80.3 %psum.15 = f32[256]{0:T(256)S(1)} all-reduce(f32[256]{0:T(256)S(1)} %convert_reduce_fusion), channel_id=1, replica_groups=mesh['lat'=8,'lon'=32] {'lat','lon'}, use_global_device_ids=true, to_apply=%region_8.9 | all-reduce | flops 256 | bytes 2048 | tf_op jit(solution)/shard_map/psum | solution.py:274
  195.3 2.0 copy.102
  199.2 2.0 copy.126
  201.2 2.3 copy.124
  203.5 2.3 copy.125
  205.9 2.4 copy.128
  211.1 4.4 %collective-permute-done.6 = f32[64,20,1]{0,2,1:T(1,128)S(1)} collective-permute-done((f32[64,20,1]{0,2,1:T(1,128)S(1)}, f32[64,20,1]{0,2,1:T(1,128)S(1)}, u32[]{:S(2)}, u32[]{:S(2)}) %collective-permute-start.6) | collective-permute-done | bytes 5152 | tf_op jit(solution)/shard_map/ppermute | solution.py:18
  223.8 116.5 %all-reduce.19.cloned.1.call-done = f32[256,720]{0,1:T(8,128)} async-done(((f32[256,720]{0,1:T(8,128)}), f32[256,720]{0,1:T(8,128)}) %all-reduce.19.cloned.1.call-update) | async-done | bytes 737296 | tf_op jit(solution)/shard_map/psum | solution.py:274
  340.3 2.0 broadcast_multiply_fusion
  343.9 2.2 gather_fusion.3
  (170 shorter events, 63.2 us)
Async XLA Ops:
  7.2 7.1 %copy-start.20 = (s32[1,256]{1,0:T(1,128)S(1)}, s32[1,256]{1,0:T(1,128)}, u32[]{:S(2)}) copy-start(s32[1,256]{1,0:T(1,128)} %param.23) | copy-start | bytes 3076
  7.2 7.1 %copy-start.19 = (s32[1,256]{1,0:T(1,128)S(1)}, s32[1,256]{1,0:T(1,128)}, u32[]{:S(2)}) copy-start(s32[1,256]{1,0:T(1,128)} %param.22) | copy-start | bytes 3076
  7.2 8.5 %copy-start.15 = (bf16[64,16,128]{2,1,0:T(8,128)(2,1)S(1)}, bf16[64,16,128]{2,1,0:T(8,128)(2,1)}, u32[]{:S(2)}) copy-start(bf16[64,16,128]{2,1,0:T(8,128)(2,1)} %param.19) | copy-start | bytes 786436
  7.2 333.1 %all-reduce.19.cloned.1.call-start = ((), (), s32[]{:S(2)}) async-start(), calls=%async_computation.1 | async-start | bytes 1474560 | tf_op jit(solution)/shard_map/psum | solution.py:274
  9.7 6.5 %copy-start.16 = (bf16[64,16,128]{2,1,0:T(8,128)(2,1)S(1)}, bf16[64,16,128]{2,1,0:T(8,128)(2,1)}, u32[]{:S(2)}) copy-start(bf16[64,16,128]{2,1,0:T(8,128)(2,1)} %param.20) | copy-start | bytes 786436
  9.8 10.1 %collective-permute-start = (bf16[80,1,128]{0,2,1:T(8,128)(2,1)S(1)}, bf16[80,1,128]{0,2,1:T(8,128)(2,1)S(1)}, u32[]{:S(2)}, u32[]{:S(2)}) collective-permute-start(bf16[80,1,128]{0,2,1:T(8,128)(2,1)S(1)} %get-tuple-element.99), channel_id=1, source_target_pairs={{0,32},{32,64},{64,96},{96,128},{128,160},{160,192},{192,224},{224... | collective-permute-start | bytes 61448 | tf_op jit(solution)/shard_map/ppermute | solution.py:18
  14.2 5.7 %collective-permute-start.1 = (bf16[80,1,128]{0,2,1:T(8,128)(2,1)S(1)}, bf16[80,1,128]{0,2,1:T(8,128)(2,1)S(1)}, u32[]{:S(2)}, u32[]{:S(2)}) collective-permute-start(bf16[80,1,128]{0,2,1:T(8,128)(2,1)S(1)} %get-tuple-element.100), channel_id=1, source_target_pairs={{32,0},{64,32},{96,64},{128,96},{160,128},{192,160},{224,192},{0,2... | collective-permute-start | bytes 61448 | tf_op jit(solution)/shard_map/ppermute | solution.py:20
  16.0 1.6 copy-start.17
  20.0 16.7 %collective-permute-start.2 = (bf16[80,18,1]{0,2,1:T(2,128)(2,1)S(1)}, bf16[80,18,1]{0,2,1:T(2,128)(2,1)S(1)}, u32[]{:S(2)}, u32[]{:S(2)}) collective-permute-start(bf16[80,18,1]{0,2,1:T(2,128)(2,1)S(1)} %get-tuple-element.97), channel_id=1, source_target_pairs={{0,1},{1,2},{2,3},{3,4},{4,5},{5,6},{6,7},{7,8},{8,9},{9,10},{10,1... | collective-permute-start | bytes 8648 | tf_op jit(solution)/shard_map/ppermute | solution.py:18
  21.4 15.3 %collective-permute-start.3 = (bf16[80,18,1]{0,2,1:T(2,128)(2,1)S(1)}, bf16[80,18,1]{0,2,1:T(2,128)(2,1)S(1)}, u32[]{:S(2)}, u32[]{:S(2)}) collective-permute-start(bf16[80,18,1]{0,2,1:T(2,128)(2,1)S(1)} %get-tuple-element.98), channel_id=1, source_target_pairs={{1,0},{2,1},{3,2},{4,3},{5,4},{6,5},{7,6},{8,7},{9,8},{10,9},{11,1... | collective-permute-start | bytes 8648 | tf_op jit(solution)/shard_map/ppermute | solution.py:20
  63.3 3.0 copy-start.13
  63.5 2.9 copy-start.12
  64.2 2.2 copy-start.11
  64.2 2.2 copy-start.10
  66.3 1.0 copy-start.18
  66.3 1.0 copy-start.22
  67.3 1.0 copy-start.9
  71.3 1.9 copy-start.6
  71.3 8.5 %copy-start = (bf16[8,64,256]{2,1,0:T(8,128)(2,1)}, bf16[8,64,256]{2,1,0:T(8,128)(2,1)S(1)}, u32[]{:S(2)}) copy-start(bf16[8,64,256]{2,1,0:T(8,128)(2,1)S(1)} %get-tuple-element.84) | copy-start | bytes 786436
  71.3 8.5 %copy-start.2 = (bf16[8,64,256]{2,1,0:T(8,128)(2,1)}, bf16[8,64,256]{2,1,0:T(8,128)(2,1)S(1)}, u32[]{:S(2)}) copy-start(bf16[8,64,256]{2,1,0:T(8,128)(2,1)S(1)} %get-tuple-element.85) | copy-start | bytes 786436
  71.3 8.5 %copy-start.4 = (bf16[8,64,256]{2,1,0:T(8,128)(2,1)}, bf16[8,64,256]{2,1,0:T(8,128)(2,1)S(1)}, u32[]{:S(2)}) copy-start(bf16[8,64,256]{2,1,0:T(8,128)(2,1)S(1)} %get-tuple-element.86) | copy-start | bytes 786436
  75.4 4.4 %copy-start.7 = (bf16[8,64,256]{2,1,0:T(8,128)(2,1)S(1)}, bf16[8,64,256]{2,1,0:T(8,128)(2,1)}, u32[]{:S(2)}) copy-start(bf16[8,64,256]{2,1,0:T(8,128)(2,1)} %copy-done.6) | copy-start | bytes 786436
  75.4 266.9 %all-to-all-start = ((f32[32,64,256]{2,1,0:T(8,128)}), f32[32,64,256]{2,1,0:T(8,128)S(1)}, u32[]{:S(2)}, u32[]{:S(2)}) async-start(f32[32,64,256]{2,1,0:T(8,128)} %broadcast_select_fusion), calls=%async_computation | async-start | bytes 4194304 | tf_op jit(solution)/shard_map/all_to_all | solution.py:269
  104.3 4.7 %copy-start.21 = (pred[16]{0:T(512)(128)(4,1)S(1)}, pred[16]{0:T(512)(128)(4,1)}, u32[]{:S(2)}) copy-start(pred[16]{0:T(512)(128)(4,1)} %constant.228.clone.1) | copy-start | bytes 52
  110.4 3.8 %copy-start.1 = (bf16[8,64,256]{2,1,0:T(8,128)(2,1)S(1)}, bf16[8,64,256]{2,1,0:T(8,128)(2,1)}, u32[]{:S(2)}) copy-start(bf16[8,64,256]{2,1,0:T(8,128)(2,1)} %copy-done) | copy-start | bytes 786436
  110.4 3.8 %copy-start.3 = (bf16[8,64,256]{2,1,0:T(8,128)(2,1)S(1)}, bf16[8,64,256]{2,1,0:T(8,128)(2,1)}, u32[]{:S(2)}) copy-start(bf16[8,64,256]{2,1,0:T(8,128)(2,1)} %copy-done.2) | copy-start | bytes 786436
  110.4 3.8 %copy-start.5 = (bf16[8,64,256]{2,1,0:T(8,128)(2,1)S(1)}, bf16[8,64,256]{2,1,0:T(8,128)(2,1)}, u32[]{:S(2)}) copy-start(bf16[8,64,256]{2,1,0:T(8,128)(2,1)} %copy-done.4) | copy-start | bytes 786436
  110.4 3.8 %copy-start.8 = (bf16[8,64,256]{2,1,0:T(8,128)(2,1)S(1)}, bf16[8,64,256]{2,1,0:T(8,128)(2,1)}, u32[]{:S(2)}) copy-start(bf16[8,64,256]{2,1,0:T(8,128)(2,1)} %copy-done.6) | copy-start | bytes 786436
  111.3 96.9 %collective-permute-start.4 = (f32[64,1,130]{0,2,1:T(8,128)}, f32[64,1,130]{0,2,1:T(8,128)S(1)}, u32[]{:S(2)}, u32[]{:S(2)}) collective-permute-start(f32[64,1,130]{0,2,1:T(8,128)} %get-tuple-element.93), channel_id=1, source_target_pairs={{0,32},{32,64},{64,96},{96,128},{128,160},{160,192},{192,224},{224... | collective-permute-start | bytes 99848 | tf_op jit(solution)/shard_map/ppermute | solution.py:18
  114.2 94.0 %collective-permute-start.5 = (f32[64,1,130]{0,2,1:T(8,128)}, f32[64,1,130]{0,2,1:T(8,128)S(1)}, u32[]{:S(2)}, u32[]{:S(2)}) collective-permute-start(f32[64,1,130]{0,2,1:T(8,128)} %get-tuple-element.94), channel_id=1, source_target_pairs={{32,0},{64,32},{96,64},{128,96},{160,128},{192,160},{224,192},{0,2... | collective-permute-start | bytes 99848 | tf_op jit(solution)/shard_map/ppermute | solution.py:20
  208.3 8.9 %collective-permute-start.7 = (f32[64,20,1]{0,2,1:T(1,128)S(1)}, f32[64,20,1]{0,2,1:T(1,128)S(1)}, u32[]{:S(2)}, u32[]{:S(2)}) collective-permute-start(f32[64,20,1]{0,2,1:T(1,128)S(1)} %get-tuple-element.91), channel_id=1, source_target_pairs={{1,0},{2,1},{3,2},{4,3},{5,4},{6,5},{7,6},{8,7},{9,8},{10,9},{11,1... | collective-permute-start | bytes 15368 | tf_op jit(solution)/shard_map/ppermute | solution.py:20
  208.8 6.7 %collective-permute-start.6 = (f32[64,20,1]{0,2,1:T(1,128)S(1)}, f32[64,20,1]{0,2,1:T(1,128)S(1)}, u32[]{:S(2)}, u32[]{:S(2)}) collective-permute-start(f32[64,20,1]{0,2,1:T(1,128)S(1)} %get-tuple-element.92), channel_id=1, source_target_pairs={{0,1},{1,2},{2,3},{3,4},{4,5},{5,6},{6,7},{7,8},{8,9},{9,10},{10,1... | collective-permute-start | bytes 15368 | tf_op jit(solution)/shard_map/ppermute | solution.py:18
  (1 other events, 1.0 us)
Sparse Core Ops, SparseCore 0:
  73.3 266.9 all-reduce.18
where the time goes:
time: 357 us; the launch traced here: 354 us
  waiting for transfers between devices  121 us (34%)
  local copies, waits for them, and re-layouts  92 us (26%)
  blocking collectives  80.3 us (22%)
  other arithmetic  21.2 us (6%)
  starting transfers between devices  19.9 us (6%)
  between operations  14.7 us (4%)
  matrix products  4.62 us (1%)
    psum x1, waiting for transfers between devices, body(): totals = lax.psum((weight_part, bias_part), ('lat', 'lon'))  117 us
    psum x1, blocking collectives, body(): totals = lax.psum((weight_part, bias_part), ('lat', 'lon'))  80.3 us
    slice x10, local copies, waits for them, and re-layouts, tile_step(): spread[:, row_off * 3 + col_off]  22.7 us
    unnamed x62, local copies, waits for them, and re-layouts  13.4 us
    reshape x9, local copies, waits for them, and re-layouts, tile_step(): tap_list.append(tile_grid[:, :, row_off:row_off + side_cells, col_off:col...  13.1 us
    slice x10, local copies, waits for them, and re-layouts, tile_step(): tile_grid[:, :, row_off:row_off + side_cells, col_off:col_off + side_cells]  11.2 us
    ppermute x4, starting transfers between devices, extended_2(): lax.ppermute(tail, axis, [(i, (i + 1) % count) for i in range(count)])  9.77 us
  transfers between devices with their start and end apart: 10, of which 2 were waited for; matrix products, arithmetic and copies ran while one was open for 21% of the time, Pallas kernels for 0%

commit v1 on v0

v1 whole, which is shorter than its diff:
```python
import functools
import math

import jax
import jax.numpy as jnp
from jax import lax
from jax.experimental import pallas as pl
from jax.experimental.pallas import tpu as pltpu
from jax.sharding import PartitionSpec as P

MESH = pl.DeviceIdType.MESH
F32 = jnp.float32
BF16 = jnp.bfloat16
ROWS = 16
LANES = 128
INP = 16
HID = 64
CH = 80
GATES = 256
TAP3 = 240
CAP = 4
TILES = 8
HALF = 384


def lane_iota(rows):
    return lax.broadcasted_iota(jnp.int32, (rows, LANES), 1)


def row_of(i):
    return pl.ds(pl.multiple_of(i * LANES, LANES), LANES)


def sigmoid(x):
    return 0.5 * jnp.tanh(0.5 * x) + 0.5


def step_kernel(
    nlat,
    nlon,
    forcing,
    hidden,
    cell,
    grad_h,
    grad_c,
    wet,
    owner,
    w_ref,
    b_ref,
    hid_o,
    cg_o,
    cn_o,
    hg_o,
    ge_o,
    ag_o,
    f32f,
    f32h,
    f32c,
    f32gh,
    f32gc,
    hid32,
    e,
    wp,
    wt,
    bcol,
    delta,
    crow,
    tiles,
    slots,
    recv,
    g32,
    wgs,
    rsr,
    las,
    lar,
    ags,
    hs,
    hr,
    gs,
    h_send,
    h_recv,
    g_send,
    g_recv,
    a_send,
    a_recv,
    r_send,
    r_recv,
    l_send,
    l_recv,
    q_send,
    q_recv,
    slot_tab,
    work_tab,
):
    lat = lax.axis_index("lat")
    lon = lax.axis_index("lon")
    up = lax.rem(lat + nlat - 1, nlat)
    down = lax.rem(lat + 1, nlat)
    left = lax.rem(lon + nlon - 1, nlon)
    right = lax.rem(lon + 1, nlon)

    def lon_peer(k):
        return lax.rem(lon + k, nlon)

    def lat_peer(k):
        return lax.rem(lat + k, nlat)

    diagonals = ((up, left), (up, right), (down, left), (down, right))

    barrier = pltpu.get_barrier_semaphore()
    for place in diagonals:
        pl.semaphore_signal(barrier, inc=1, device_id=place, device_id_type=MESH)

    def greet_lat(k, c):
        pl.semaphore_signal(barrier, inc=1, device_id=(lat_peer(k), lon), device_id_type=MESH)
        return c

    lax.fori_loop(1, nlat, greet_lat, 0)

    def greet_lon(k, c):
        pl.semaphore_signal(barrier, inc=1, device_id=(lat, lon_peer(k)), device_id_type=MESH)
        return c

    lax.fori_loop(1, nlon, greet_lon, 0)

    f32f[...] = forcing[...].astype(F32).reshape(INP * ROWS, LANES)
    f32h[...] = hidden[...].astype(F32).reshape(HID * ROWS, LANES)
    lane80 = lane_iota(CH)

    def field_row(i):
        return jnp.concatenate(
            [f32f[pl.ds(i, INP, stride=ROWS), :], f32h[pl.ds(i, HID, stride=ROWS), :]], 0
        )

    edge_l = jnp.zeros((CH, LANES), F32)
    edge_r = jnp.zeros((CH, LANES), F32)
    for i in range(ROWS):
        row = field_row(i)
        e[CH : 2 * CH, (i + 1) * LANES : (i + 2) * LANES] = row.astype(BF16)
        e[0:CH, (i + 1) * LANES : (i + 2) * LANES] = pltpu.roll(row, 1, 1).astype(BF16)
        e[2 * CH : TAP3, (i + 1) * LANES : (i + 2) * LANES] = pltpu.roll(
            row, LANES - 1, 1
        ).astype(BF16)
        edge_l = jnp.where(lane80 == i, row[:, 0:1], edge_l)
        edge_r = jnp.where(lane80 == i, row[:, LANES - 1 : LANES], edge_r)
        if i == 0:
            hs[0] = row.astype(BF16)
        if i == ROWS - 1:
            hs[1] = row.astype(BF16)
    hs[2] = edge_l.astype(BF16)
    hs[3] = edge_r.astype(BF16)

    pl.semaphore_wait(barrier, nlon - 1 + nlat - 1 + 4)

    halo_plan = (
        (1, 0, (down, lon)),
        (0, 1, (up, lon)),
        (3, 2, (lat, right)),
        (2, 3, (lat, left)),
        (1, 4, (down, right)),
        (1, 5, (down, left)),
        (0, 6, (up, right)),
        (0, 7, (up, left)),
    )
    halo = []
    for src, dst, place in halo_plan:
        copy = pltpu.make_async_remote_copy(
            src_ref=hs.at[src],
            dst_ref=hr.at[dst],
            send_sem=h_send.at[dst],
            recv_sem=h_recv.at[dst],
            device_id=place,
            device_id_type=MESH,
        )
        copy.start()
        halo.append(copy)

    f32c[...] = cell[...].astype(F32).reshape(HID * ROWS, LANES)
    f32gh[...] = grad_h[...].astype(F32).reshape(HID * ROWS, LANES)
    f32gc[...] = grad_c[...].astype(F32).reshape(HID * ROWS, LANES)
    lane256 = lax.broadcasted_iota(jnp.int32, (GATES, GATES), 1)
    w_all = jnp.concatenate(
        [w_ref[...].astype(F32), jnp.zeros((GATES, 3 * GATES - 3 * TAP3), F32)], 1
    )
    for dr in range(3):
        part = w_all if dr == 0 else pltpu.roll(w_all, 3 * GATES - dr * TAP3, 1)
        part = jnp.where(lane256 < TAP3, part[:, :GATES], 0.0)
        wp[dr] = part.astype(BF16)
        wt[dr] = part.T.astype(BF16)
    bcol[...] = jnp.broadcast_to(b_ref[...], (LANES, GATES)).T
    ones_row = lax.broadcasted_iota(jnp.int32, (GATES - TAP3, 18 * LANES), 0) == 0
    e[TAP3:GATES, :] = jnp.where(ones_row, 1.0, 0.0).astype(BF16)
    delta[:, 0 : 2 * LANES] = jnp.zeros((GATES, 2 * LANES), BF16)
    delta[:, 18 * LANES : 20 * LANES] = jnp.zeros((GATES, 2 * LANES), BF16)

    base = lon * TILES
    wet_here = [wet[0, base + q] for q in range(TILES)]
    own_here = [owner[0, base + q] for q in range(TILES)]

    def plan_slot(o, c):
        source = jnp.int32(0)
        for q in range(TILES):
            source = source + jnp.where((wet_here[q] > 0) & (own_here[q] == o), q, 0)
        slot_tab[o] = source
        return c

    lax.fori_loop(0, nlon, plan_slot, 0)

    def plan_work(d, carry):
        count, work = carry
        has = jnp.int32(0)
        for q in range(TILES):
            has = has + jnp.where(
                (wet[0, d * TILES + q] > 0) & (owner[0, d * TILES + q] == lon), 1, 0
            )
        work = tuple(
            work[r] + jnp.where((has > 0) & (count == r), d, 0) for r in range(CAP)
        )
        return (count + has, work)

    _, work = lax.fori_loop(
        0, nlon, plan_work, (jnp.int32(0), tuple(jnp.int32(0) for _ in range(CAP)))
    )
    for r in range(CAP):
        work_tab[r] = work[r]

    lane64 = lane_iota(HID)
    live = jnp.zeros((HID, LANES), F32)
    for q in range(TILES):
        live = jnp.where(
            lane64 // 16 == q, jnp.where(wet_here[q] > 0, 1.0, 0.0).astype(F32), live
        )

    for copy in halo:
        copy.wait()

    keep_up = jnp.where(lat > 0, 1.0, 0.0).astype(F32)
    keep_down = jnp.where(lat < nlat - 1, 1.0, 0.0).astype(F32)
    from_left = hr[2].astype(F32)
    from_right = hr[3].astype(F32)
    for i in range(ROWS):
        cols = slice((i + 1) * LANES, (i + 2) * LANES)
        a = e[0:CH, cols].astype(F32)
        e[0:CH, cols] = jnp.where(
            lane80 == 0, pltpu.roll(from_left, (LANES - i) % LANES, 1), a
        ).astype(BF16)
        a = e[2 * CH : TAP3, cols].astype(F32)
        e[2 * CH : TAP3, cols] = jnp.where(
            lane80 == LANES - 1, pltpu.roll(from_right, LANES - 1 - i, 1), a
        ).astype(BF16)
    for block, keep, mid, lft, rgt in ((0, keep_up, 0, 4, 5), (17, keep_down, 1, 6, 7)):
        cols = slice(block * LANES, (block + 1) * LANES)
        row = hr[mid].astype(F32)
        e[CH : 2 * CH, cols] = (row * keep).astype(BF16)
        a = jnp.where(
            lane80 == 0, pltpu.roll(hr[lft].astype(F32), 1, 1), pltpu.roll(row, 1, 1)
        )
        e[0:CH, cols] = (a * keep).astype(BF16)
        a = jnp.where(
            lane80 == LANES - 1,
            pltpu.roll(hr[rgt].astype(F32), LANES - 1, 1),
            pltpu.roll(row, LANES - 1, 1),
        )
        e[2 * CH : TAP3, cols] = (a * keep).astype(BF16)

    def forward(c, carry):
        pre = jnp.zeros((GATES, 2 * LANES), F32)
        for dr in range(3):
            cols = pl.ds(pl.multiple_of(c * 2 * LANES + dr * LANES, LANES), 2 * LANES)
            pre = pre + jnp.dot(wp[dr], e[:, cols], preferred_element_type=F32)
        for s in range(2):
            i = c * 2 + s
            full = pre[:, s * LANES : (s + 1) * LANES] + bcol[...]
            g_in = sigmoid(full[0:HID])
            g_forget = sigmoid(full[HID : 2 * HID])
            g_out = sigmoid(full[2 * HID : 3 * HID])
            cand = jnp.tanh(full[3 * HID :])
            old = f32c[pl.ds(i, HID, stride=ROWS), :]
            new = g_forget * old + g_in * cand
            squash = jnp.tanh(new)
            crow[i] = new
            hid32[pl.ds(i, HID, stride=ROWS), :] = live * g_out * squash
            back_h = live * f32gh[pl.ds(i, HID, stride=ROWS), :]
            back_c = live * f32gc[pl.ds(i, HID, stride=ROWS), :] + back_h * g_out * (
                1.0 - squash * squash
            )
            cell_back = back_c * g_forget
            cg_o[pl.ds(i, HID, stride=ROWS), :] = cell_back
            back_in = back_c * g_in
            cols = row_of(i + 2)
            delta[0:HID, cols] = (back_in * cand * (1.0 - g_in)).astype(BF16)
            delta[HID : 2 * HID, cols] = (cell_back * old * (1.0 - g_forget)).astype(BF16)
            delta[2 * HID : 3 * HID, cols] = (
                back_h * squash * g_out * (1.0 - g_out)
            ).astype(BF16)
            delta[3 * HID :, cols] = (back_in * (1.0 - cand * cand)).astype(BF16)
        return carry

    lax.fori_loop(0, ROWS // 2, forward, 0)

    lane16 = lane_iota(16) // 16

    def regroup(step, carry):
        half = step // 4
        subs = pl.ds(pl.multiple_of(lax.rem(step, 4) * 16, 16), 16)
        x = [crow[half * 8 + k, subs, :] for k in range(8)]
        for s in (1, 2, 4):
            low = (lane16 // s) % 2 == 0
            y = list(x)
            for k in range(8):
                if (k // s) % 2 == 0:
                    a, b = x[k], x[k + s]
                    y[k] = jnp.where(low, a, pltpu.roll(b, 16 * s, 1))
                    y[k + s] = jnp.where(low, pltpu.roll(a, LANES - 16 * s, 1), b)
            x = y
        for q in range(8):
            tiles[q, subs, row_of(half)] = x[q].astype(BF16)
        return carry

    lax.fori_loop(0, 8, regroup, 0)

    def fill(o, carry):
        slots[o] = tiles[slot_tab[o]]
        return carry

    lax.fori_loop(0, nlon, fill, 0)
    recv[lon] = slots[lon]

    def tile_copy(k):
        peer = lon_peer(k)
        return pltpu.make_async_remote_copy(
            src_ref=slots.at[peer],
            dst_ref=recv.at[lon],
            send_sem=a_send.at[k],
            recv_sem=a_recv.at[k],
            device_id=(lat, peer),
            device_id_type=MESH,
        )

    def start_tile(k, c):
        tile_copy(k).start()
        return c

    for dr in range(3):
        g32[:, dr * GATES : (dr + 1) * GATES] = lax.dot_general(
            delta[:, 2 * LANES : 18 * LANES],
            e[:, dr * LANES : (dr + ROWS) * LANES],
            (((1,), (1,)), ((), ())),
            preferred_element_type=F32,
        )
    per = GATES // nlon

    def pack_terms(k, carry):
        rows = pl.ds(pl.multiple_of(k * per, per), per)
        wgs[k] = jnp.concatenate([g32[rows, :HALF], g32[rows, HALF:]], 0).astype(BF16)
        return carry

    lax.fori_loop(0, nlon, pack_terms, 0)
    rsr[lon] = wgs[lon]

    def scatter_copy(k):
        peer = lon_peer(k)
        return pltpu.make_async_remote_copy(
            src_ref=wgs.at[peer],
            dst_ref=rsr.at[lon],
            send_sem=r_send.at[k],
            recv_sem=r_recv.at[k],
            device_id=(lat, peer),
            device_id_type=MESH,
        )

    def start_scatter(k, c):
        scatter_copy(k).start()
        return c

    lax.fori_loop(1, nlon, start_scatter, 0)
    lax.fori_loop(1, nlon, start_tile, 0)

    colv_l = jnp.zeros((HID, LANES), F32)
    colv_r = jnp.zeros((HID, LANES), F32)
    for c in range(9):
        acc = jnp.zeros((GATES, 2 * LANES), F32)
        for dr in range(3):
            start = (2 * c + 2 - dr) * LANES
            acc = acc + jnp.dot(
                wt[dr], delta[:, start : start + 2 * LANES], preferred_element_type=F32
            )
        for s in range(2):
            r = 2 * c + s
            part = acc[:, s * LANES : (s + 1) * LANES]
            s0 = part[INP:CH]
            s1 = part[CH + INP : 2 * CH]
            s2 = part[2 * CH + INP : TAP3]
            colv_l = jnp.where(lane64 == r, s0[:, 0:1], colv_l)
            colv_r = jnp.where(lane64 == r, s2[:, LANES - 1 : LANES], colv_r)
            total = (
                s1
                + jnp.where(lane64 < LANES - 1, pltpu.roll(s0, LANES - 1, 1), 0.0)
                + jnp.where(lane64 > 0, pltpu.roll(s2, 1, 1), 0.0)
            )
            if r == 0:
                gs[0] = total.astype(BF16)
            elif r == 17:
                gs[1] = total.astype(BF16)
            else:
                hg_o[r - 1] = total
    gs[2] = colv_l.astype(BF16)
    gs[3] = colv_r.astype(BF16)
    grad_plan = (
        (1, 0, (down, lon)),
        (0, 1, (up, lon)),
        (3, 2, (lat, right)),
        (2, 3, (lat, left)),
        (3, 4, (down, right)),
        (2, 5, (down, left)),
        (3, 6, (up, right)),
        (2, 7, (up, left)),
    )
    edges = []
    for src, dst, place in grad_plan:
        copy = pltpu.make_async_remote_copy(
            src_ref=gs.at[src],
            dst_ref=ge_o.at[dst],
            send_sem=g_send.at[dst],
            recv_sem=g_recv.at[dst],
            device_id=place,
            device_id_type=MESH,
        )
        copy.start()
        edges.append(copy)
    hid_o[...] = hid32[...].reshape(HID, ROWS, LANES).astype(BF16)

    def wait_scatter(k, c):
        scatter_copy(k).wait()
        return c

    lax.fori_loop(1, nlon, wait_scatter, 0)
    lon_sum = lax.fori_loop(
        0, nlon, lambda k, t: t + rsr[k].astype(F32), jnp.zeros((2 * per, HALF), F32)
    )
    las[...] = lon_sum
    lar[lat] = lon_sum

    def lat_copy(k):
        peer = lat_peer(k)
        return pltpu.make_async_remote_copy(
            src_ref=las,
            dst_ref=lar.at[lat],
            send_sem=l_send.at[k],
            recv_sem=l_recv.at[k],
            device_id=(peer, lon),
            device_id_type=MESH,
        )

    for k in range(1, nlat):
        lat_copy(k).start()
    for k in range(1, nlat):
        lat_copy(k).wait()
    total = lar[0]
    for k in range(1, nlat):
        total = total + lar[k]
    ags[...] = total.astype(BF16)
    ag_o[lon] = total.astype(BF16)

    def gather_copy(k):
        peer = lon_peer(k)
        return pltpu.make_async_remote_copy(
            src_ref=ags,
            dst_ref=ag_o.at[lon],
            send_sem=q_send.at[k],
            recv_sem=q_recv.at[k],
            device_id=(lat, peer),
            device_id_type=MESH,
        )

    def start_gather(k, c):
        gather_copy(k).start()
        return c

    lax.fori_loop(1, nlon, start_gather, 0)

    def wait_tile(k, c):
        tile_copy(k).wait()
        return c

    lax.fori_loop(1, nlon, wait_tile, 0)
    for r in range(CAP):
        cn_o[r] = recv[work_tab[r]].astype(F32)
    for copy in edges:
        copy.wait()

    def wait_gather(k, c):
        gather_copy(k).wait()
        return c

    lax.fori_loop(1, nlon, wait_gather, 0)


def finish_kernel(
    nlat, nlon, scaling, hid, cg, cn, hg, ge, ag, hid_o, cn_o, hg_o, cg_o, wg_o, bg_o
):
    lat = lax.axis_index("lat")
    hid_o[...] = hid[...]
    cg_o[...] = cg[...]
    cn_o[...] = cn[...]
    lane64 = lane_iota(HID)
    keep_up = jnp.where(lat > 0, 1.0, 0.0).astype(F32)
    keep_down = jnp.where(lat < nlat - 1, 1.0, 0.0).astype(F32)
    left = ge[2].astype(F32)
    right = ge[3].astype(F32)
    for i in range(ROWS):
        row = hg[i]
        add_l = pltpu.roll(left, (LANES - 1 - i) % LANES, 1)
        add_r = pltpu.roll(right, LANES - 2 - i, 1)
        if i == 0:
            row = row + keep_up * ge[0].astype(F32)
            add_l = add_l + keep_up * pltpu.roll(ge[4].astype(F32), LANES - 17, 1)
            add_r = add_r + keep_up * pltpu.roll(ge[5].astype(F32), LANES - 18, 1)
        if i == ROWS - 1:
            row = row + keep_down * ge[1].astype(F32)
            add_l = add_l + keep_down * ge[6].astype(F32)
            add_r = add_r + keep_down * pltpu.roll(ge[7].astype(F32), LANES - 1, 1)
        row = row + jnp.where(lane64 == 0, add_l, jnp.where(lane64 == LANES - 1, add_r, 0.0))
        hg_o[pl.ds(i, HID, stride=ROWS), :] = row
    per = GATES // nlon
    bias = []
    for k in range(nlon):
        x = ag[k].astype(F32) * scaling
        whole = jnp.concatenate([x[:per], x[per:]], 1)
        wg_o[k * per : (k + 1) * per, :] = jnp.concatenate(
            [whole[:, d * GATES : d * GATES + TAP3] for d in range(3)], 1
        )
        bias.append(whole[:, LANES:GATES])
    bg_o[...] = jnp.concatenate(bias, 0).T[TAP3 - LANES : TAP3 - LANES + 1, :]


def body(forcing, hidden, cell, grad_hidden, grad_cell, wet_mask, tile_owner, w_gates, b_gates):
    nlat = lax.axis_size("lat")
    nlon = lax.axis_size("lon")
    per = GATES // nlon
    vmem = pl.BlockSpec(memory_space=pltpu.VMEM)
    smem = pl.BlockSpec(memory_space=pltpu.SMEM)
    cells = HID * ROWS
    sems = pltpu.SemaphoreType.DMA
    hid, cg, cn, hg, ge, ag = pl.pallas_call(
        functools.partial(step_kernel, nlat, nlon),
        out_shape=(
            jax.ShapeDtypeStruct((HID, ROWS, LANES), BF16),
            jax.ShapeDtypeStruct((cells, LANES), F32),
            jax.ShapeDtypeStruct((CAP, HID, 256), F32),
            jax.ShapeDtypeStruct((ROWS, HID, LANES), F32),
            jax.ShapeDtypeStruct((8, HID, LANES), BF16),
            jax.ShapeDtypeStruct((nlon, 2 * per, HALF), BF16),
        ),
        in_specs=[vmem] * 5 + [smem] * 2 + [vmem] * 2,
        out_specs=[vmem] * 6,
        scratch_shapes=[
            pltpu.VMEM((INP * ROWS, LANES), F32),
            pltpu.VMEM((cells, LANES), F32),
            pltpu.VMEM((cells, LANES), F32),
            pltpu.VMEM((cells, LANES), F32),
            pltpu.VMEM((cells, LANES), F32),
            pltpu.VMEM((cells, LANES), F32),
            pltpu.VMEM((GATES, 18 * LANES), BF16),
            pltpu.VMEM((3, GATES, GATES), BF16),
            pltpu.VMEM((3, GATES, GATES), BF16),
            pltpu.VMEM((GATES, LANES), F32),
            pltpu.VMEM((GATES, 20 * LANES), BF16),
            pltpu.VMEM((ROWS, HID, LANES), F32),
            pltpu.VMEM((TILES, HID, 256), BF16),
            pltpu.VMEM((nlon, HID, 256), BF16),
            pltpu.VMEM((nlon, HID, 256), BF16),
            pltpu.VMEM((GATES, 2 * HALF), F32),
            pltpu.VMEM((nlon, 2 * per, HALF), BF16),
            pltpu.VMEM((nlon, 2 * per, HALF), BF16),
            pltpu.VMEM((2 * per, HALF), F32),
            pltpu.VMEM((nlat, 2 * per, HALF), F32),
            pltpu.VMEM((2 * per, HALF), BF16),
            pltpu.VMEM((4, CH, LANES), BF16),
            pltpu.VMEM((8, CH, LANES), BF16),
            pltpu.VMEM((4, HID, LANES), BF16),
            sems((8,)),
            sems((8,)),
            sems((8,)),
            sems((8,)),
            sems((nlon,)),
            sems((nlon,)),
            sems((nlon,)),
            sems((nlon,)),
            sems((nlat,)),
            sems((nlat,)),
            sems((nlon,)),
            sems((nlon,)),
            pltpu.SMEM((nlon,), jnp.int32),
            pltpu.SMEM((CAP,), jnp.int32),
        ],
        compiler_params=pltpu.CompilerParams(
            collective_id=0, has_side_effects=True, vmem_limit_bytes=48 << 20
        ),
        name="step",
    )(
        forcing,
        hidden,
        cell,
        grad_hidden,
        grad_cell,
        wet_mask,
        tile_owner,
        w_gates,
        b_gates.reshape(1, GATES),
    )
    scaling = 1.0 / math.sqrt(float(nlat * nlon * CAP * 256))
    hid, cn, hg, cg, wg, bg = pl.pallas_call(
        functools.partial(finish_kernel, nlat, nlon, scaling),
        out_shape=(
            jax.ShapeDtypeStruct((HID, ROWS, LANES), BF16),
            jax.ShapeDtypeStruct((CAP, HID, 256), F32),
            jax.ShapeDtypeStruct((cells, LANES), F32),
            jax.ShapeDtypeStruct((cells, LANES), F32),
            jax.ShapeDtypeStruct((GATES, 3 * TAP3), F32),
            jax.ShapeDtypeStruct((1, GATES), F32),
        ),
        in_specs=[vmem] * 6,
        out_specs=[vmem] * 6,
        name="finish",
    )(hid, cg, cn, hg, ge, ag)
    return (
        hid,
        cn,
        hg.reshape(HID, ROWS, LANES),
        cg.reshape(HID, ROWS, LANES),
        wg,
        bg.reshape(GATES),
    )


def solution(mesh):
    return jax.shard_map(
        body,
        mesh=mesh,
        in_specs=(
            P(None, "lat", "lon"),
            P(None, "lat", "lon"),
            P(None, "lat", "lon"),
            P(None, "lat", "lon"),
            P(None, "lat", "lon"),
            P("lat", None),
            P("lat", None),
            P(),
            P(),
        ),
        out_specs=(
            P(None, "lat", "lon"),
            P(("lat", "lon"), None, None),
            P(None, "lat", "lon"),
            P(None, "lat", "lon"),
            P(),
            P(),
        ),
        check_vma=False,
    )
```

time: 357 us -> 72.3 us (0.20)
  waiting for transfers between devices: 121 us -> 0 us
  local copies, waits for them, and re-layouts: 92 us -> 9.77 us
  blocking collectives: 80.3 us -> 0 us
  Pallas kernels: 0 us -> 61.5 us
  other arithmetic: 21.2 us -> 0 us
  starting transfers between devices: 19.9 us -> 0 us
  between operations: 14.7 us -> 0.77 us
  matrix products: 4.62 us -> 0 us
    psum x1 -> x0, waiting for transfers between devices: 117 us -> none  [body(): totals = lax.psum((weight_part, bias_part), ('lat', 'lon'))]
    psum x1 -> x0, blocking collectives: 80.3 us -> none  [body(): totals = lax.psum((weight_part, bias_part), ('lat', 'lon'))]
    pallas_call x0 -> x2, Pallas kernels: none -> 61.5 us  [the longest x1 58.1 us: body(): pl.pallas_call(functools.partial(step_kernel, nlat, nlon), out_shape=(jax...]
    slice x25 -> x0, local copies, waits for them, and re-layouts: 37.2 us -> none  [the longest x10 22.7 us: tile_step(): spread[:, row_off * 3 + col_off]]
    ppermute x8 -> x0, starting transfers between devices: 15.5 us -> none  [the longest x4 9.77 us: extended_2(): lax.ppermute(tail, axis, [(i, (i + 1) % count) for i in range(count)])]
    reshape x10 -> x0, local copies, waits for them, and re-layouts: 13.1 us -> none  [the longest x9 13.1 us: tile_step(): tap_list.append(tile_grid[:, :, row_off:row_off + side_cells, col_off:col...]
    convert_element_type x9 -> x0, local copies, waits for them, and re-layouts: 12.1 us -> none  [the longest x2 3.86 us: lstm_terms(): back_h = live_cells * hidden_cot.astype(jnp.float32)]
    transpose x2 -> x0, other arithmetic: 4.99 us -> none  [the longest x1 4.72 us: fold_grad(): across = fold_edges(jnp.transpose(shaped, (0, 2, 3, 1, 4)))]
  transfers between devices with their start and end apart: 10 -> 0, of which waited for: 2 -> 0; matrix products, arithmetic and copies ran while one was open for 21% -> 0% of each run, Pallas kernels for 0% -> 0%
where the time goes in v1:
time: 72.3 us; the launch traced here: 72.1 us
  Pallas kernels  61.5 us (85%)
  local copies, waits for them, and re-layouts  9.77 us (14%)
  between operations  0.77 us (1%)
    pallas_call x1, Pallas kernels, body(): pl.pallas_call(functools.partial(step_kernel, nlat, nlon), out_shape=(jax...  58.1 us
    unnamed x30, local copies, waits for them, and re-layouts  9.77 us
    pallas_call x1, Pallas kernels, body(): pl.pallas_call(functools.partial(finish_kernel, nlat, nlon, scaling), out...  3.41 us

profile of v1, /device:TPU:1, one launch (start us, length us, event | category | flops | bytes accessed | tf_op | source)
XLA Modules:
  0.0 72.1 jit_solution(4914078001638770649)
XLA Ops:
  0.6 0.0 copy-start.3
  0.6 0.0 copy-start.4
  0.7 0.0 copy-start.10
  0.7 0.0 copy-start.11
  0.7 0.0 copy-start.12
  0.7 0.0 copy-start.13
  0.7 1.2 %copy.15.w_ref = bf16[256,720]{1,0:T(8,128)(2,1)S(1)} copy(bf16[256,720]{0,1:T(8,128)(2,1)} %param.16) | data formatting | bytes 737280 | tf_op args[7]
  1.9 0.0 copy-done.3
  1.9 0.0 copy-done.4
  1.9 0.0 copy-done.10
  1.9 0.0 copy-done.11
  1.9 0.0 copy-done.12
  2.0 0.0 copy-done.13
  2.0 0.0 copy-start.5
  2.0 0.9 %copy-done.5 = bf16[64,16,128]{2,1,0:T(8,128)(2,1)S(1)} copy-done((bf16[64,16,128]{2,1,0:T(8,128)(2,1)S(1)}, bf16[64,16,128]{2,1,0:T(8,128)(2,1)}, u32[]{:S(2)}) %copy-start.5) | copy-done | bytes 262168
  2.9 0.0 copy-start.6
  2.9 0.9 %copy-done.6 = bf16[64,16,128]{2,1,0:T(8,128)(2,1)S(1)} copy-done((bf16[64,16,128]{2,1,0:T(8,128)(2,1)S(1)}, bf16[64,16,128]{2,1,0:T(8,128)(2,1)}, u32[]{:S(2)}) %copy-start.6) | copy-done | bytes 262168
  3.9 58.1 %step.1 = (bf16[64,16,128]{2,1,0:T(8,128)(2,1)S(1)}, f32[1024,128]{1,0:T(8,128)S(1)}, f32[4,64,256]{2,1,0:T(8,128)S(1)}, f32[16,64,128]{2,1,0:T(8,128)S(1)}, bf1...) custom-call(bf16[16,16,128]{2,1,0:T(8,128)(2,1)S(1)} %copy-done.10, bf16[64,16,128]{2,1,0:T(8,128)(2,1)S(1)} %copy-done.3, ...), custom_call_target="tpu_custom_call" | custom-call | tf_op jit(solution)/shard_map/step/pallas_call | solution.py:545
  62.0 0.0 copy-start
  62.0 0.8 %copy-done = f32[1024,128]{1,0:T(8,128)} copy-done((f32[1024,128]{1,0:T(8,128)}, f32[1024,128]{1,0:T(8,128)S(1)}, u32[]{:S(2)}) %copy-start) | copy-done | bytes 524312
  62.8 0.0 copy-start.1
  62.8 0.8 %copy-done.1 = f32[16,64,128]{2,1,0:T(8,128)} copy-done((f32[16,64,128]{2,1,0:T(8,128)}, f32[16,64,128]{2,1,0:T(8,128)S(1)}, u32[]{:S(2)}) %copy-start.1) | copy-done | bytes 524312
  63.6 0.0 copy-start.2
  63.6 0.7 %copy-done.2 = bf16[32,16,384]{2,1,0:T(8,128)(2,1)} copy-done((bf16[32,16,384]{2,1,0:T(8,128)(2,1)}, bf16[32,16,384]{2,1,0:T(8,128)(2,1)S(1)}, u32[]{:S(2)}) %copy-start.2) | copy-done | bytes 393240
  64.4 0.0 copy-start.7
  64.4 0.7 copy-done.7
  65.1 0.0 copy-start.8
  65.1 0.7 copy-done.8
  65.8 0.0 copy-start.9
  65.8 0.6 copy-done.9
  66.4 3.4 %finish.1 = (bf16[64,16,128]{2,1,0:T(8,128)(2,1)}, f32[4,64,256]{2,1,0:T(8,128)}, f32[1024,128]{1,0:T(8,128)}, f32[1024,128]{1,0:T(8,128)}, f32[256,720]{1,0:T(8,128)}, /*index=5*/f32[1,256]{1,0:T(1,128)}) custom-call(bf16[64,16,128]{2,1,0:T(8,128)(2,1)} %copy-done.7, f32[1024,128]{1,0:T(8,128)} %copy-done, f32[4,64,256]{2,1,0:T(8,128)} %copy-done.8, ...), custom_call_target="tpu_custom_call" | custom-call | tf_op jit(solution)/shard_map/finish/pallas_call | solution.py:613
  69.8 2.3 %copy.16 = f32[256,720]{0,1:T(8,128)} copy(f32[256,720]{1,0:T(8,128)} %get-tuple-element.34) | data formatting | bytes 1474560
Async XLA Ops:
  0.6 1.3 %copy-start.3 = (bf16[64,16,128]{2,1,0:T(8,128)(2,1)S(1)}, bf16[64,16,128]{2,1,0:T(8,128)(2,1)}, u32[]{:S(2)}) copy-start(bf16[64,16,128]{2,1,0:T(8,128)(2,1)} %hidden.1) | copy-start | bytes 786436
  0.6 1.3 %copy-start.4 = (bf16[64,16,128]{2,1,0:T(8,128)(2,1)S(1)}, bf16[64,16,128]{2,1,0:T(8,128)(2,1)}, u32[]{:S(2)}) copy-start(bf16[64,16,128]{2,1,0:T(8,128)(2,1)} %cell.1) | copy-start | bytes 786436
  0.7 1.3 %copy-start.10 = (bf16[16,16,128]{2,1,0:T(8,128)(2,1)S(1)}, bf16[16,16,128]{2,1,0:T(8,128)(2,1)}, u32[]{:S(2)}) copy-start(bf16[16,16,128]{2,1,0:T(8,128)(2,1)} %forcing.1) | copy-start | bytes 196612
  0.7 1.3 %copy-start.11 = (s32[1,256]{1,0:T(1,128)S(1)}, s32[1,256]{1,0:T(1,128)}, u32[]{:S(2)}) copy-start(s32[1,256]{1,0:T(1,128)} %wet.1) | copy-start | bytes 3076
  0.7 1.3 %copy-start.12 = (s32[1,256]{1,0:T(1,128)S(1)}, s32[1,256]{1,0:T(1,128)}, u32[]{:S(2)}) copy-start(s32[1,256]{1,0:T(1,128)} %owner.1) | copy-start | bytes 3076
  0.7 1.3 %copy-start.13 = (f32[256]{0:T(256)S(1)}, f32[256]{0:T(256)}, u32[]{:S(2)}) copy-start(f32[256]{0:T(256)} %param.17) | copy-start | bytes 3076
  2.0 1.0 %copy-start.5 = (bf16[64,16,128]{2,1,0:T(8,128)(2,1)S(1)}, bf16[64,16,128]{2,1,0:T(8,128)(2,1)}, u32[]{:S(2)}) copy-start(bf16[64,16,128]{2,1,0:T(8,128)(2,1)} %grad_h.1) | copy-start | bytes 786436
  2.9 0.9 %copy-start.6 = (bf16[64,16,128]{2,1,0:T(8,128)(2,1)S(1)}, bf16[64,16,128]{2,1,0:T(8,128)(2,1)}, u32[]{:S(2)}) copy-start(bf16[64,16,128]{2,1,0:T(8,128)(2,1)} %grad_c.1) | copy-start | bytes 786436
  62.0 0.8 %copy-start = (f32[1024,128]{1,0:T(8,128)}, f32[1024,128]{1,0:T(8,128)S(1)}, u32[]{:S(2)}) copy-start(f32[1024,128]{1,0:T(8,128)S(1)} %get-tuple-element.19.cg) | copy-start | bytes 1572868
  62.8 0.8 %copy-start.1 = (f32[16,64,128]{2,1,0:T(8,128)}, f32[16,64,128]{2,1,0:T(8,128)S(1)}, u32[]{:S(2)}) copy-start(f32[16,64,128]{2,1,0:T(8,128)S(1)} %get-tuple-element.21.hg) | copy-start | bytes 1572868
  63.6 0.7 %copy-start.2 = (bf16[32,16,384]{2,1,0:T(8,128)(2,1)}, bf16[32,16,384]{2,1,0:T(8,128)(2,1)S(1)}, u32[]{:S(2)}) copy-start(bf16[32,16,384]{2,1,0:T(8,128)(2,1)S(1)} %get-tuple-element.23.ag) | copy-start | bytes 1179652
  64.4 0.7 copy-start.7
  65.1 0.7 copy-start.8
  65.8 0.7 copy-start.9

commit v2 on v1

--- a/solution.py
+++ b/solution.py
@@ -20,7 +20,10 @@
 TAP3 = 240
 CAP = 4
 TILES = 8
-HALF = 384
+PADK = 768
+
+
+BATCHES = (0, 7, 10, 19, 26, 31)
 
 
 def lane_iota(rows):
@@ -38,14 +41,14 @@
 def step_kernel(
     nlat,
     nlon,
-    forcing,
-    hidden,
-    cell,
-    grad_h,
-    grad_c,
+    forcing_hbm,
+    hidden_hbm,
+    cell_hbm,
+    grad_h_hbm,
+    grad_c_hbm,
     wet,
     owner,
-    w_ref,
+    w_hbm,
     b_ref,
     hid_o,
     cg_o,
@@ -53,6 +56,12 @@
     hg_o,
     ge_o,
     ag_o,
+    forcing,
+    hidden,
+    cell,
+    grad_h,
+    grad_c,
+    w_ref,
     f32f,
     f32h,
     f32c,
@@ -61,14 +70,14 @@
     hid32,
     e,
     wp,
-    wt,
     bcol,
     delta,
     crow,
     tiles,
     slots,
     recv,
-    g32,
+    halves,
+    pair_half,
     wgs,
     rsr,
     las,
@@ -77,12 +86,15 @@
     hs,
     hr,
     gs,
+    in_sem,
     h_send,
     h_recv,
     g_send,
     g_recv,
     a_send,
     a_recv,
+    c_send,
+    c_recv,
     r_send,
     r_recv,
     l_send,
@@ -90,7 +102,6 @@
     q_send,
     q_recv,
     slot_tab,
-    work_tab,
 ):
     lat = lax.axis_index("lat")
     lon = lax.axis_index("lon")
@@ -105,6 +116,29 @@
     def lat_peer(k):
         return lax.rem(lat + k, nlat)
 
+    core = lax.rem(lat, 2)
+    partner = lat + 1 - 2 * core
+    places = nlat // 2
+
+    def drain(ref, sem):
+        pltpu.make_async_copy(ref, ref, sem).wait()
+
+    loads = [
+        pltpu.make_async_copy(src, dst, in_sem.at[k])
+        for k, (src, dst) in enumerate(
+            (
+                (forcing_hbm, forcing),
+                (hidden_hbm, hidden),
+                (cell_hbm, cell),
+                (grad_h_hbm, grad_h),
+                (grad_c_hbm, grad_c),
+                (w_hbm, w_ref),
+            )
+        )
+    ]
+    for load in loads:
+        load.start()
+
     diagonals = ((up, left), (up, right), (down, left), (down, right))
 
     barrier = pltpu.get_barrier_semaphore()
@@ -123,6 +157,8 @@
 
     lax.fori_loop(1, nlon, greet_lon, 0)
 
+    loads[0].wait()
+    loads[1].wait()
     f32f[...] = forcing[...].astype(F32).reshape(INP * ROWS, LANES)
     f32h[...] = hidden[...].astype(F32).reshape(HID * ROWS, LANES)
     lane80 = lane_iota(CH)
@@ -175,18 +211,20 @@
         copy.start()
         halo.append(copy)
 
+    for load in loads[2:]:
+        load.wait()
     f32c[...] = cell[...].astype(F32).reshape(HID * ROWS, LANES)
     f32gh[...] = grad_h[...].astype(F32).reshape(HID * ROWS, LANES)
     f32gc[...] = grad_c[...].astype(F32).reshape(HID * ROWS, LANES)
-    lane256 = lax.broadcasted_iota(jnp.int32, (GATES, GATES), 1)
-    w_all = jnp.concatenate(
-        [w_ref[...].astype(F32), jnp.zeros((GATES, 3 * GATES - 3 * TAP3), F32)], 1
-    )
     for dr in range(3):
-        part = w_all if dr == 0 else pltpu.roll(w_all, 3 * GATES - dr * TAP3, 1)
-        part = jnp.where(lane256 < TAP3, part[:, :GATES], 0.0)
-        wp[dr] = part.astype(BF16)
-        wt[dr] = part.T.astype(BF16)
+        part = jnp.concatenate(
+            [
+                w_ref[dr * TAP3 : (dr + 1) * TAP3, :].astype(F32),
+                jnp.zeros((GATES - TAP3, GATES), F32),
+            ],
+            0,
+        )
+        wp[dr] = part.T.astype(BF16)
     bcol[...] = jnp.broadcast_to(b_ref[...], (LANES, GATES)).T
     ones_row = lax.broadcasted_iota(jnp.int32, (GATES - TAP3, 18 * LANES), 0) == 0
     e[TAP3:GATES, :] = jnp.where(ones_row, 1.0, 0.0).astype(BF16)
@@ -205,24 +243,6 @@
         return c
 
     lax.fori_loop(0, nlon, plan_slot, 0)
-
-    def plan_work(d, carry):
-        count, work = carry
-        has = jnp.int32(0)
-        for q in range(TILES):
-            has = has + jnp.where(
-                (wet[0, d * TILES + q] > 0) & (owner[0, d * TILES + q] == lon), 1, 0
-            )
-        work = tuple(
-            work[r] + jnp.where((has > 0) & (count == r), d, 0) for r in range(CAP)
-        )
-        return (count + has, work)
-
-    _, work = lax.fori_loop(
-        0, nlon, plan_work, (jnp.int32(0), tuple(jnp.int32(0) for _ in range(CAP)))
-    )
-    for r in range(CAP):
-        work_tab[r] = work[r]
 
     lane64 = lane_iota(HID)
     live = jnp.zeros((HID, LANES), F32)
@@ -331,59 +351,57 @@
         return pltpu.make_async_remote_copy(
             src_ref=slots.at[peer],
             dst_ref=recv.at[lon],
-            send_sem=a_send.at[k],
-            recv_sem=a_recv.at[k],
+            send_sem=a_send,
+            recv_sem=a_recv,
             device_id=(lat, peer),
             device_id_type=MESH,
         )
 
-    def start_tile(k, c):
-        tile_copy(k).start()
-        return c
+    def start_tiles(first, last):
+        def start(k, c):
+            tile_copy(k).start()
+            return c
+
+        lax.fori_loop(first, last, start, 0)
+
+    cuts = [1 + (nlon - 1) * n // 31 for n in BATCHES]
+    start_tiles(cuts[0], cuts[1])
 
     for dr in range(3):
-        g32[:, dr * GATES : (dr + 1) * GATES] = lax.dot_general(
+        rows = TAP3 if dr < 2 else GATES
+        terms = lax.dot_general(
+            e[0:rows, dr * LANES : (dr + ROWS) * LANES],
             delta[:, 2 * LANES : 18 * LANES],
-            e[:, dr * LANES : (dr + ROWS) * LANES],
             (((1,), (1,)), ((), ())),
             preferred_element_type=F32,
         )
-    per = GATES // nlon
-
-    def pack_terms(k, carry):
-        rows = pl.ds(pl.multiple_of(k * per, per), per)
-        wgs[k] = jnp.concatenate([g32[rows, :HALF], g32[rows, HALF:]], 0).astype(BF16)
-        return carry
-
-    lax.fori_loop(0, nlon, pack_terms, 0)
-    rsr[lon] = wgs[lon]
-
-    def scatter_copy(k):
-        peer = lon_peer(k)
-        return pltpu.make_async_remote_copy(
-            src_ref=wgs.at[peer],
-            dst_ref=rsr.at[lon],
-            send_sem=r_send.at[k],
-            recv_sem=r_recv.at[k],
-            device_id=(lat, peer),
-            device_id_type=MESH,
-        )
-
-    def start_scatter(k, c):
-        scatter_copy(k).start()
-        return c
-
-    lax.fori_loop(1, nlon, start_scatter, 0)
-    lax.fori_loop(1, nlon, start_tile, 0)
+        for half in range(2):
+            halves[half, dr * TAP3 : dr * TAP3 + rows, :] = terms[
+                :, half * LANES : (half + 1) * LANES
+            ]
+    filler = 2 * TAP3 + GATES
+    halves[:, filler:PADK, :] = jnp.zeros((2, PADK - filler, LANES), F32)
+    pair = pltpu.make_async_remote_copy(
+        src_ref=halves.at[1 - core],
+        dst_ref=pair_half,
+        send_sem=c_send.at[0],
+        recv_sem=c_recv.at[0],
+        device_id=(partner, lon),
+        device_id_type=MESH,
+    )
+    pair.start()
+    start_tiles(cuts[1], cuts[2])
 
     colv_l = jnp.zeros((HID, LANES), F32)
     colv_r = jnp.zeros((HID, LANES), F32)
     for c in range(9):
-        acc = jnp.zeros((GATES, 2 * LANES), F32)
+        acc = jnp.zeros((TAP3, 2 * LANES), F32)
         for dr in range(3):
             start = (2 * c + 2 - dr) * LANES
             acc = acc + jnp.dot(
-                wt[dr], delta[:, start : start + 2 * LANES], preferred_element_type=F32
+                w_ref[dr * TAP3 : (dr + 1) * TAP3, :],
+                delta[:, start : start + 2 * LANES],
+                preferred_element_type=F32,
             )
         for s in range(2):
             r = 2 * c + s
@@ -428,72 +446,108 @@
         )
         copy.start()
         edges.append(copy)
+    per = PADK // nlon
+    pair.wait()
+
+    def pack_terms(k, carry):
+        rows = pl.ds(pl.multiple_of(k * per, per), per)
+        wgs[k] = (halves[core, rows, :] + pair_half[rows, :]).astype(BF16)
+        return carry
+
+    lax.fori_loop(0, nlon, pack_terms, 0, unroll=4)
+    rsr[lon] = wgs[lon]
+
+    def start_scatter(k, c):
+        peer = lon_peer(k)
+        pltpu.make_async_remote_copy(
+            src_ref=wgs.at[peer],
+            dst_ref=rsr.at[lon],
+            send_sem=r_send,
+            recv_sem=r_recv,
+            device_id=(lat, peer),
+            device_id_type=MESH,
+        ).start()
+        return c
+
+    lax.fori_loop(1, nlon, start_scatter, 0)
+    start_tiles(cuts[2], cuts[3])
     hid_o[...] = hid32[...].reshape(HID, ROWS, LANES).astype(BF16)
 
-    def wait_scatter(k, c):
-        scatter_copy(k).wait()
-        return c
-
-    lax.fori_loop(1, nlon, wait_scatter, 0)
+    def plan_work(d, carry):
+        count, work = carry
+        has = jnp.int32(0)
+        for q in range(TILES):
+            has = has + jnp.where(
+                (wet[0, d * TILES + q] > 0) & (owner[0, d * TILES + q] == lon), 1, 0
+            )
+        work = tuple(
+            work[r] + jnp.where((has > 0) & (count == r), d, 0) for r in range(CAP)
+        )
+        return (count + has, work)
+
+    _, work = lax.fori_loop(
+        0, nlon, plan_work, (jnp.int32(0), tuple(jnp.int32(0) for _ in range(CAP)))
+    )
+
+    drain(rsr.at[pl.ds(0, nlon - 1)], r_recv)
     lon_sum = lax.fori_loop(
-        0, nlon, lambda k, t: t + rsr[k].astype(F32), jnp.zeros((2 * per, HALF), F32)
+        0, nlon, lambda k, t: t + rsr[k].astype(F32), jnp.zeros((per, LANES), F32), unroll=4
     )
     las[...] = lon_sum
-    lar[lat] = lon_sum
-
-    def lat_copy(k):
-        peer = lat_peer(k)
-        return pltpu.make_async_remote_copy(
+    lar[lat // 2] = lon_sum
+    across = []
+    for k in range(1, places):
+        copy = pltpu.make_async_remote_copy(
             src_ref=las,
-            dst_ref=lar.at[lat],
+            dst_ref=lar.at[lat // 2],
             send_sem=l_send.at[k],
             recv_sem=l_recv.at[k],
-            device_id=(peer, lon),
+            device_id=(lat_peer(2 * k), lon),
             device_id_type=MESH,
         )
-
-    for k in range(1, nlat):
-        lat_copy(k).start()
-    for k in range(1, nlat):
-        lat_copy(k).wait()
+        copy.start()
+        across.append(copy)
+    start_tiles(cuts[3], cuts[4])
+    for copy in across:
+        copy.wait()
     total = lar[0]
-    for k in range(1, nlat):
+    for k in range(1, places):
         total = total + lar[k]
     ags[...] = total.astype(BF16)
-    ag_o[lon] = total.astype(BF16)
-
-    def gather_copy(k):
-        peer = lon_peer(k)
-        return pltpu.make_async_remote_copy(
+    ag_o[core, lon] = total.astype(BF16)
+
+    def start_gather(k, c):
+        pltpu.make_async_remote_copy(
             src_ref=ags,
-            dst_ref=ag_o.at[lon],
-            send_sem=q_send.at[k],
-            recv_sem=q_recv.at[k],
-            device_id=(lat, peer),
+            dst_ref=ag_o.at[core, lon],
+            send_sem=q_send,
+            recv_sem=q_recv,
+            device_id=(lat, lon_peer(k)),
             device_id_type=MESH,
-        )
-
-    def start_gather(k, c):
-        gather_copy(k).start()
+        ).start()
         return c
 
     lax.fori_loop(1, nlon, start_gather, 0)
-
-    def wait_tile(k, c):
-        tile_copy(k).wait()
-        return c
-
-    lax.fori_loop(1, nlon, wait_tile, 0)
-    for r in range(CAP):
-        cn_o[r] = recv[work_tab[r]].astype(F32)
+    start_tiles(cuts[4], cuts[5])
     for copy in edges:
         copy.wait()
-
-    def wait_gather(k, c):
-        gather_copy(k).wait()
-        return c
-
-    lax.fori_loop(1, nlon, wait_gather, 0)
+    drain(ag_o.at[core, pl.ds(0, nlon - 1)], q_recv)
+    last = pltpu.make_async_remote_copy(
+        src_ref=ag_o.at[core],
+        dst_ref=ag_o.at[core],
+        send_sem=c_send.at[1],
+        recv_sem=c_recv.at[1],
+        device_id=(partner, lon),
+        device_id_type=MESH,
+    )
+    last.start()
+    drain(recv.at[pl.ds(0, nlon - 1)], a_recv)
+    for r in range(CAP):
+        cn_o[r] = recv[work[r]].astype(F32)
+    drain(rsr.at[pl.ds(0, nlon - 1)], r_send)
+    drain(ag_o.at[core, pl.ds(0, nlon - 1)], q_send)
+    drain(recv.at[pl.ds(0, nlon - 1)], a_send)
+    last.wait()
 
 
 def finish_kernel(
@@ -522,25 +576,26 @@
             add_r = add_r + keep_down * pltpu.roll(ge[7].astype(F32), LANES - 1, 1)
         row = row + jnp.where(lane64 == 0, add_l, jnp.where(lane64 == LANES - 1, add_r, 0.0))
         hg_o[pl.ds(i, HID, stride=ROWS), :] = row
-    per = GATES // nlon
-    bias = []
-    for k in range(nlon):
-        x = ag[k].astype(F32) * scaling
-        whole = jnp.concatenate([x[:per], x[per:]], 1)
-        wg_o[k * per : (k + 1) * per, :] = jnp.concatenate(
-            [whole[:, d * GATES : d * GATES + TAP3] for d in range(3)], 1
-        )
-        bias.append(whole[:, LANES:GATES])
-    bg_o[...] = jnp.concatenate(bias, 0).T[TAP3 - LANES : TAP3 - LANES + 1, :]
+    low = ag[0].astype(F32).reshape(PADK, LANES) * scaling
+    high = ag[1].astype(F32).reshape(PADK, LANES) * scaling
+    wg_o[:, :LANES] = low[: 3 * TAP3]
+    wg_o[:, LANES:] = high[: 3 * TAP3]
+    bg_o[:, :LANES] = low[3 * TAP3 : 3 * TAP3 + 1]
+    bg_o[:, LANES:] = high[3 * TAP3 : 3 * TAP3 + 1]
 
 
 def body(forcing, hidden, cell, grad_hidden, grad_cell, wet_mask, tile_owner, w_gates, b_gates):
     nlat = lax.axis_size("lat")
     nlon = lax.axis_size("lon")
-    per = GATES // nlon
+    per = PADK // nlon
+    anyw = pl.BlockSpec(memory_space=pltpu.HBM)
     vmem = pl.BlockSpec(memory_space=pltpu.VMEM)
     smem = pl.BlockSpec(memory_space=pltpu.SMEM)
     cells = HID * ROWS
+
+    def in_hbm(x):
+        return pltpu.with_memory_space_constraint(x, pltpu.HBM)
+
     sems = pltpu.SemaphoreType.DMA
     hid, cg, cn, hg, ge, ag = pl.pallas_call(
         functools.partial(step_kernel, nlat, nlon),
@@ -550,11 +605,17 @@
             jax.ShapeDtypeStruct((CAP, HID, 256), F32),
             jax.ShapeDtypeStruct((ROWS, HID, LANES), F32),
             jax.ShapeDtypeStruct((8, HID, LANES), BF16),
-            jax.ShapeDtypeStruct((nlon, 2 * per, HALF), BF16),
+            jax.ShapeDtypeStruct((2, nlon, per, LANES), BF16),
         ),
-        in_specs=[vmem] * 5 + [smem] * 2 + [vmem] * 2,
+        in_specs=[anyw] * 5 + [smem] * 2 + [anyw, vmem],
         out_specs=[vmem] * 6,
         scratch_shapes=[
+            pltpu.VMEM((INP, ROWS, LANES), BF16),
+            pltpu.VMEM((HID, ROWS, LANES), BF16),
+            pltpu.VMEM((HID, ROWS, LANES), BF16),
+            pltpu.VMEM((HID, ROWS, LANES), BF16),
+            pltpu.VMEM((HID, ROWS, LANES), BF16),
+            pltpu.VMEM((3 * TAP3, GATES), BF16),
             pltpu.VMEM((INP * ROWS, LANES), F32),
             pltpu.VMEM((cells, LANES), F32),
             pltpu.VMEM((cells, LANES), F32),
@@ -563,50 +624,52 @@
             pltpu.VMEM((cells, LANES), F32),
             pltpu.VMEM((GATES, 18 * LANES), BF16),
             pltpu.VMEM((3, GATES, GATES), BF16),
-            pltpu.VMEM((3, GATES, GATES), BF16),
             pltpu.VMEM((GATES, LANES), F32),
             pltpu.VMEM((GATES, 20 * LANES), BF16),
             pltpu.VMEM((ROWS, HID, LANES), F32),
             pltpu.VMEM((TILES, HID, 256), BF16),
             pltpu.VMEM((nlon, HID, 256), BF16),
             pltpu.VMEM((nlon, HID, 256), BF16),
-            pltpu.VMEM((GATES, 2 * HALF), F32),
-            pltpu.VMEM((nlon, 2 * per, HALF), BF16),
-            pltpu.VMEM((nlon, 2 * per, HALF), BF16),
-            pltpu.VMEM((2 * per, HALF), F32),
-            pltpu.VMEM((nlat, 2 * per, HALF), F32),
-            pltpu.VMEM((2 * per, HALF), BF16),
+            pltpu.VMEM((2, PADK, LANES), F32),
+            pltpu.VMEM((PADK, LANES), F32),
+            pltpu.VMEM((nlon, per, LANES), BF16),
+            pltpu.VMEM((nlon, per, LANES), BF16),
+            pltpu.VMEM((per, LANES), F32),
+            pltpu.VMEM((nlat // 2, per, LANES), F32),
+            pltpu.VMEM((per, LANES), BF16),
             pltpu.VMEM((4, CH, LANES), BF16),
             pltpu.VMEM((8, CH, LANES), BF16),
             pltpu.VMEM((4, HID, LANES), BF16),
+            sems((6,)),
             sems((8,)),
             sems((8,)),
             sems((8,)),
             sems((8,)),
-            sems((nlon,)),
-            sems((nlon,)),
-            sems((nlon,)),
-            sems((nlon,)),
-            sems((nlat,)),
-            sems((nlat,)),
-            sems((nlon,)),
-            sems((nlon,)),
+            sems,
+            sems,
+            sems((2,)),
+            sems((2,)),
+            sems,
+            sems,
+            sems((nlat // 2,)),
+            sems((nlat // 2,)),
+            sems,
+            sems,
             pltpu.SMEM((nlon,), jnp.int32),
-            pltpu.SMEM((CAP,), jnp.int32),
         ],
         compiler_params=pltpu.CompilerParams(
-            collective_id=0, has_side_effects=True, vmem_limit_bytes=48 << 20
+            collective_id=0, has_side_effects=True, vmem_limit_bytes=40 << 20
         ),
         name="step",
     )(
-        forcing,
-        hidden,
-        cell,
-        grad_hidden,
-        grad_cell,
+        in_hbm(forcing),
+        in_hbm(hidden),
+        in_hbm(cell),
+        in_hbm(grad_hidden),
+        in_hbm(grad_cell),
         wet_mask,
         tile_owner,
-        w_gates,
+        in_hbm(w_gates.T),
         b_gates.reshape(1, GATES),
     )
     scaling = 1.0 / math.sqrt(float(nlat * nlon * CAP * 256))
@@ -617,11 +680,12 @@
             jax.ShapeDtypeStruct((CAP, HID, 256), F32),
             jax.ShapeDtypeStruct((cells, LANES), F32),
             jax.ShapeDtypeStruct((cells, LANES), F32),
-            jax.ShapeDtypeStruct((GATES, 3 * TAP3), F32),
+            jax.ShapeDtypeStruct((3 * TAP3, GATES), F32),
             jax.ShapeDtypeStruct((1, GATES), F32),
         ),
         in_specs=[vmem] * 6,
         out_specs=[vmem] * 6,
+        compiler_params=pltpu.CompilerParams(vmem_limit_bytes=12 << 20),
         name="finish",
     )(hid, cg, cn, hg, ge, ag)
     return (
@@ -629,7 +693,7 @@
         cn,
         hg.reshape(HID, ROWS, LANES),
         cg.reshape(HID, ROWS, LANES),
-        wg,
+        wg.T,
         bg.reshape(GATES),
     )
 

time: 72.3 us -> 54.4 us (0.75)
  local copies, waits for them, and re-layouts: 9.77 us -> 0.69 us
  Pallas kernels: 61.5 us -> 52.9 us
    unnamed x30 -> x6, local copies, waits for them, and re-layouts: 9.77 us -> 0.69 us
    pallas_call x1, Pallas kernels: 58.1 us -> 51.3 us  [body(): pl.pallas_call(functools.partial(step_kernel, nlat, nlon), out_shape=(jax...]
    pallas_call x1, Pallas kernels: 3.41 us -> 1.65 us  [body(): pl.pallas_call(functools.partial(finish_kernel, nlat, nlon, scaling), out...]
where the time goes in v2:
time: 54.4 us; the launch traced here: 54.3 us
  Pallas kernels  52.9 us (97%)
  local copies, waits for them, and re-layouts  0.69 us (1%)
  between operations  0.67 us (1%)
    pallas_call x1, Pallas kernels, body(): pl.pallas_call(functools.partial(step_kernel, nlat, nlon), out_shape=(jax...  51.3 us
    pallas_call x1, Pallas kernels, body(): pl.pallas_call(functools.partial(finish_kernel, nlat, nlon, scaling), out...  1.65 us

profile of v2, /device:TPU:1, one launch (start us, length us, event | category | flops | bytes accessed | tf_op | source)
XLA Modules:
  0.0 54.3 jit_solution(3037429764614376258)
XLA Ops:
  0.6 0.0 copy-start.1
  0.6 0.0 copy-start.2
  0.7 0.0 copy-start
  0.7 0.7 %copy-done.1 = s32[1,256]{1,0:T(1,128)S(1)} copy-done((s32[1,256]{1,0:T(1,128)S(1)}, s32[1,256]{1,0:T(1,128)}, u32[]{:S(2)}) %copy-start.1) | copy-done | bytes 1048
  1.3 0.0 copy-done.2
  1.3 0.0 copy-done
  1.3 51.3 %step.1 = (bf16[64,16,128]{2,1,0:T(8,128)(2,1)S(1)}, f32[1024,128]{1,0:T(8,128)S(1)}, f32[4,64,256]{2,1,0:T(8,128)S(1)}, f32[16,64,128]{2,1,0:T(8,128)S(1)}, bf1...) custom-call(bf16[16,16,128]{2,1,0:T(8,128)(2,1)} %forcing_hbm.1, bf16[64,16,128]{2,1,0:T(8,128)(2,1)} %hidden_hbm.1, ...), custom_call_target="tpu_custom_call" | custom-call | tf_op jit(solution)/shard_map/step/pallas_call | solution.py:600
  52.6 1.7 %finish.1 = (bf16[64,16,128]{2,1,0:T(8,128)(2,1)}, f32[4,64,256]{2,1,0:T(8,128)}, f32[1024,128]{1,0:T(8,128)}, f32[1024,128]{1,0:T(8,128)}, f32[720,256]{1,0:T(8,128)}, /*index=5*/f32[1,256]{1,0:T(1,128)}) custom-call(bf16[64,16,128]{2,1,0:T(8,128)(2,1)S(1)} %get-tuple-element.18.hid, f32[1024,128]{1,0:T(8,128)S(1)} %get-tuple-element.19.cg, ...), custom_call_target="tpu_custom_call" | custom-call | tf_op jit(solution)/shard_map/finish/pallas_call | solution.py:676
Async XLA Ops:
  0.6 0.7 %copy-start.1 = (s32[1,256]{1,0:T(1,128)S(1)}, s32[1,256]{1,0:T(1,128)}, u32[]{:S(2)}) copy-start(s32[1,256]{1,0:T(1,128)} %owner.1) | copy-start | bytes 3076
  0.6 0.7 %copy-start.2 = (f32[256]{0:T(256)S(1)}, f32[256]{0:T(256)}, u32[]{:S(2)}) copy-start(f32[256]{0:T(256)} %param.17) | copy-start | bytes 3076
  0.7 0.7 %copy-start = (s32[1,256]{1,0:T(1,128)S(1)}, s32[1,256]{1,0:T(1,128)}, u32[]{:S(2)}) copy-start(s32[1,256]{1,0:T(1,128)} %wet.1) | copy-start | bytes 3076
